TPU v7x, 256 devices: a whole 4x4x8 slice. The times are simulated.
256 devices in a mesh: pipe: 8 (over x_lo, y), expert: 32 (over z, x_hi, core).
Axes of the slice: x: 4 (x_hi: 2, x_lo: 2; x = x_hi * 2 + x_lo), y: 4, z: 8, core: 2. Of those that a mesh axis runs over, the one named last changes fastest.
Arguments:
- tokens: bfloat16 [8, 4096, 2048], P('pipe', 'expert'), may hold values from -6 to 6
- routes: int32 [8, 4096, 6], P('pipe', 'expert'), may hold values from 0 to 31, all different within a row; in each aligned block of 128 rows (0 to 127, 128 to 255, ..., all dimensions but the last counted through in order) at most 36 rows name the same one
- norm_gain: float32 [8, 2048], P('pipe'), may hold values from 0.1 to 1.9
- router_weight: bfloat16 [8, 2048, 32], P('pipe'), may hold values from -0.125 to 0.125
- w_gate: bfloat16 [8, 32, 2048, 768], P('pipe', 'expert'), may hold values from -0.125 to 0.125
- w_up: bfloat16 [8, 32, 2048, 768], P('pipe', 'expert'), may hold values from -0.125 to 0.125
- w_down: bfloat16 [8, 32, 768, 2048], P('pipe', 'expert'), may hold values from -0.21875 to 0.21875
Outputs:
- received: bfloat16 [8, 4096, 2048], P('pipe', 'expert')
Inputs may be any that keep to these rules, and one draw needn't show every extreme that they name: Within each aligned block of 128 tokens of a section (the tokens of one device), the 6 routes of a token name different experts and no expert is named by more than 36 routes; some expert is named by exactly 36 routes in some block; every expert is named somewhere.
All inputs are finite; a program needn't handle non-finite values.
Results may differ from a plain program's by a relative error of at most 0.0039.
Values may be sent and summed in bfloat16 or wider, within the bound.
A program may use at most 128 MiB of HBM per device.

v0:
```python
import jax
import jax.numpy as jnp
from jax import lax
from jax.sharding import PartitionSpec as P


def shifted(shard, axis, by):
    devices = lax.axis_size(axis)
    return lax.ppermute(shard, axis, [(i, (i + by) % devices) for i in range(devices)])


def earlier_matrix(count):
    positions = jnp.arange(count, dtype=jnp.int32)
    return (positions[None, :] < positions[:, None]).astype(jnp.bfloat16)


def slot_ranks(route_block, experts):
    flat_routes = route_block.reshape(-1)
    hits = (flat_routes[:, None] == jnp.arange(experts, dtype=jnp.int32)[None, :]).astype(
        jnp.bfloat16
    )
    before = jnp.dot(earlier_matrix(flat_routes.shape[0]), hits, preferred_element_type=jnp.float32)
    ranks = jnp.sum(before * hits.astype(jnp.float32), axis=1).astype(jnp.int32)
    return ranks.reshape(route_block.shape)


def expert_ffn(slot_block, gate_matrix, up_matrix, down_matrix):
    gate_part = jnp.dot(slot_block, gate_matrix, preferred_element_type=jnp.float32)
    up_part = jnp.dot(slot_block, up_matrix, preferred_element_type=jnp.float32)
    hidden = (jax.nn.silu(gate_part) * up_part).astype(jnp.bfloat16)
    return jnp.dot(hidden, down_matrix, preferred_element_type=jnp.float32).astype(jnp.bfloat16)


def local(tokens, routes, norm_gain, router_weight, w_gate, w_up, w_down):
    local_rows = tokens[0]
    route_local = routes[0]
    gate_matrix = w_gate[0, 0]
    up_matrix = w_up[0, 0]
    down_matrix = w_down[0, 0]
    experts = lax.axis_size("expert")
    tok_dev, top_count = route_local.shape
    model_width = local_rows.shape[1]
    capacity = 3 * tok_dev * top_count // (2 * experts)
    wide_rows = local_rows.astype(jnp.float32)
    mean_square = jnp.mean(wide_rows * wide_rows, axis=-1, keepdims=True)
    normed = (wide_rows * lax.rsqrt(mean_square + 1e-06) * norm_gain[0]).astype(jnp.bfloat16)
    score = jax.nn.sigmoid(jnp.dot(normed, router_weight[0], preferred_element_type=jnp.float32))
    expert_ids = jnp.arange(experts, dtype=jnp.int32)
    chosen = route_local[..., None] == expert_ids[None, None, :]
    picked = jnp.sum(jnp.where(chosen, score[:, None, :], 0.0), axis=-1)
    gate_values = (picked / jnp.sum(picked, axis=1, keepdims=True)).astype(jnp.bfloat16)
    ranks = slot_ranks(route_local, experts)
    slots = route_local * capacity + ranks
    slot_hits = slots[..., None] == jnp.arange(experts * capacity, dtype=jnp.int32)[None, None, :]
    weights_map = jnp.sum(
        jnp.where(slot_hits, gate_values.astype(jnp.float32)[..., None], 0.0), axis=1
    ).astype(jnp.bfloat16)
    table = lax.all_gather(route_local, "expert", axis=0, tiled=True)
    gathered = lax.all_gather(normed, "expert", axis=0, tiled=True)
    own_index = lax.axis_index("expert")
    flat_count = tok_dev * top_count
    blocks = table.reshape(experts, flat_count)
    mine = blocks == own_index
    mine_values = mine.astype(jnp.bfloat16)
    own_ranks = jnp.dot(
        mine_values, earlier_matrix(flat_count).T, preferred_element_type=jnp.float32
    ).astype(jnp.int32)
    matches = mine[..., None] & (
        own_ranks[..., None] == jnp.arange(capacity, dtype=jnp.int32)[None, None, :]
    )
    selector = jnp.any(matches.reshape(experts, tok_dev, top_count, capacity), axis=2).astype(
        jnp.bfloat16
    )
    buffer = jnp.einsum(
        "btc,btd->bcd",
        selector,
        gathered.reshape(experts, tok_dev, model_width),
        preferred_element_type=jnp.float32,
    ).astype(jnp.bfloat16)
    owner_out = expert_ffn(buffer.reshape(-1, model_width), gate_matrix, up_matrix, down_matrix)
    returned = lax.all_to_all(
        owner_out.reshape(experts, capacity, model_width),
        "expert",
        split_axis=0,
        concat_axis=0,
        tiled=True,
    )
    moe = jnp.dot(
        weights_map,
        returned.reshape(experts * capacity, model_width),
        preferred_element_type=jnp.float32,
    )
    layer_out = (wide_rows + moe).astype(jnp.bfloat16)[None]
    received = shifted(layer_out, "pipe", 1)
    return received


def solution(mesh):
    return jax.shard_map(
        local,
        mesh=mesh,
        in_specs=(
            P("pipe", "expert", None),
            P("pipe", "expert", None),
            P("pipe", None),
            P("pipe", None, None),
            P("pipe", "expert", None, None),
            P("pipe", "expert", None, None),
            P("pipe", "expert", None, None),
        ),
        out_specs=P("pipe", "expert", None),
        check_vma=False,
    )
```

profile of v0, /device:TPU:2, one launch (start us, length us, event | category | flops | bytes accessed | tf_op | source)
XLA Modules:
  0.0 350.7 jit_solution(5233156969499989968)
XLA Ops:
  6.5 1.4 fusion.19
  7.9 2.0 fusion.21
  10.0 44.4 %all-gather = s32[1,4096,6]{1,0,2:T(1,128)S(1)} all-gather(s32[1,128,6]{1,0,2:T(1,128)} %param.8), channel_id=2, replica_groups=mesh['pipe'=8,'expert'=32] {'expert'}, dimensions={1}, use_global_device_ids=true | all-gather | bytes 101376 | tf_op jit(solution)/shard_map/all_gather | solution.py:58
  54.4 0.9 fusion.35
  55.3 1.5 copy.23
  56.8 2.5 eq.86
  59.3 1.0 fusion.14
  60.3 1.1 copy.24
  61.4 0.8 eq.87
  62.2 1.2 copy.25
  63.4 0.8 copy.33
  64.2 0.5 fusion.1
  64.7 85.4 %all-gather.3.cloned.1.call-done = bf16[4096,2048]{1,0:T(8,128)(2,1)} async-done(((bf16[128,2048]{1,0:T(8,128)(2,1)}), bf16[4096,2048]{1,0:T(8,128)(2,1)}) %all-gather.3.cloned.1.call-update) | async-done | bytes 16777232 | tf_op jit(solution)/shard_map/all_gather | solution.py:59
  150.0 10.4 %convolution_convert_fusion.1 = bf16[32,36,2048]{2,1,0:T(8,128)(2,1)} fusion(bf16[32,128,2048]{2,1,0:T(8,128)(2,1)} %bitcast.55, pred[32,128,36]{1,0,2:T(8,128)(4,1)S(1)} %fusion.1), kind=kOutput, calls=%fused_computation.1 | convolution fusion | flops 606339072 | bytes 21643264 | tf_op jit(solution)/shard_map/btc,btd->bcd/dot_general | solution.py:74
  160.4 7.2 %reshape.90 = bf16[1152,2048]{1,0:T(8,128)(2,1)} reshape(bf16[32,36,2048]{2,1,0:T(8,128)(2,1)} %convolution_convert_fusion.1) | data formatting | bytes 9437184 | tf_op jit(solution)/shard_map/reshape | solution.py:80
  167.7 6.8 %fusion.5 = f32[1152,768]{1,0:T(8,128)S(1)} fusion(bf16[1152,2048]{1,0:T(8,128)(2,1)} %reshape.90, bf16[1,1,2048,768]{3,2,1,0:T(8,128)(2,1)} %param.11), kind=kOutput, calls=%fused_computation.11 | convolution fusion | flops 3623878656 | bytes 11403264 | tf_op jit(solution)/shard_map/dot_general | solution.py:28
  174.4 4.2 %fusion.2 = bf16[1152,768]{1,0:T(8,128)(2,1)S(1)} fusion(bf16[1152,2048]{1,0:T(8,128)(2,1)S(1)} %copy-done.1, f32[1152,768]{1,0:T(8,128)S(1)} %fusion.5, bf16[1,1,2048,768]{3,2,1,0:T(8,128)(2,1)S(1)} %copy-done.4), kind=kOutput, calls=%fused_computation.8 | convolution fusion | flops 3629187072 | bytes 13172736 | tf_op jit(solution)/shard_map/dot_general | solution.py:29
  178.6 5.5 %convolution_convert_fusion = bf16[1152,2048]{1,0:T(8,128)(2,1)} fusion(bf16[1152,768]{1,0:T(8,128)(2,1)S(1)} %fusion.2, bf16[1,1,768,2048]{3,2,1,0:T(8,128)(2,1)S(1)} %copy-done), kind=kOutput, calls=%fused_computation | convolution fusion | flops 3626237952 | bytes 9633792 | tf_op jit(solution)/shard_map/dot_general | solution.py:31
  184.2 7.2 %reshape.91 = bf16[32,36,2048]{2,1,0:T(8,128)(2,1)} reshape(bf16[1152,2048]{1,0:T(8,128)(2,1)} %convolution_convert_fusion) | data formatting | bytes 9437184 | tf_op jit(solution)/shard_map/reshape | solution.py:82
  191.4 5.8 %all-to-all-start = ((bf16[32,36,2048]{2,1,0:T(8,128)(2,1)}), bf16[32,36,2048]{2,1,0:T(8,128)(2,1)}, u32[]{:S(2)}, u32[]{:S(2)}) async-start(bf16[32,36,2048]{2,1,0:T(8,128)(2,1)} %reshape.91), calls=%async_computation | async-start | bytes 10485760 | tf_op jit(solution)/shard_map/all_to_all | solution.py:81
  197.2 0.1 copy.19
  197.3 0.1 eq.73
  197.5 0.4 fusion.15
  197.8 0.1 convert_element_type.75
  198.1 1.5 fusion.18
  199.6 0.5 select_reduce_fusion
  200.1 116.3 %all-to-all-done = bf16[32,36,2048]{2,1,0:T(8,128)(2,1)} async-done(((bf16[32,36,2048]{2,1,0:T(8,128)(2,1)}), bf16[32,36,2048]{2,1,0:T(8,128)(2,1)}, u32[]{:S(2)}, u32[]{:S(2)}) %all-to-all-start) | async-done | bytes 4718624 | tf_op jit(solution)/shard_map/all_to_all | solution.py:81
  316.4 7.2 %reshape.92 = bf16[1152,2048]{1,0:T(8,128)(2,1)} reshape(bf16[32,36,2048]{2,1,0:T(8,128)(2,1)} %all-to-all-done) | data formatting | bytes 9437184 | tf_op jit(solution)/shard_map/reshape | solution.py:90
  323.6 3.3 fusion.10
  326.9 1.6 collective-permute-start
  328.5 14.5 %collective-permute-done = bf16[1,128,2048]{2,1,0:T(8,128)(2,1)S(1)} collective-permute-done((bf16[1,128,2048]{2,1,0:T(8,128)(2,1)S(1)}, bf16[1,128,2048]{2,1,0:T(8,128)(2,1)S(1)}, u32[]{:S(2)}, u32[]{:S(2)}) %collective-permute-start) | collective-permute-done | bytes 524320 | tf_op jit(solution)/shard_map/ppermute | solution.py:9
  343.0 0.8 copy.37
  (19 shorter events, 0.2 us)
Async XLA Ops:
  6.5 172.1 %copy-start = (bf16[1,1,768,2048]{3,2,1,0:T(8,128)(2,1)S(1)}, bf16[1,1,768,2048]{3,2,1,0:T(8,128)(2,1)}, u32[]{:S(2)}) copy-start(bf16[1,1,768,2048]{3,2,1,0:T(8,128)(2,1)} %param.13) | copy-start | bytes 9437188
  6.5 143.5 %all-gather.3.cloned.1.call-start = ((), (), s32[]{:S(2)}) async-start(), calls=%async_computation.1 | async-start | bytes 17301504 | tf_op jit(solution)/shard_map/all_gather | solution.py:59
  167.7 6.8 %copy-start.1 = (bf16[1152,2048]{1,0:T(8,128)(2,1)S(1)}, bf16[1152,2048]{1,0:T(8,128)(2,1)}, u32[]{:S(2)}) copy-start(bf16[1152,2048]{1,0:T(8,128)(2,1)} %reshape.90) | copy-start | bytes 14155780
  167.7 6.8 %copy-start.4 = (bf16[1,1,2048,768]{3,2,1,0:T(8,128)(2,1)S(1)}, bf16[1,1,2048,768]{3,2,1,0:T(8,128)(2,1)}, u32[]{:S(2)}) copy-start(bf16[1,1,2048,768]{3,2,1,0:T(8,128)(2,1)} %param.12) | copy-start | bytes 9437188
  191.4 5.8 %copy-start.2 = (s32[1,128,6]{1,0,2:T(1,128)S(1)}, s32[1,128,6]{1,0,2:T(1,128)}, u32[]{:S(2)}) copy-start(s32[1,128,6]{1,0,2:T(1,128)} %param.8) | copy-start | bytes 9220
  191.4 6.7 %copy-start.3 = (f32[1,2048]{1,0:T(1,128)S(1)}, f32[1,2048]{1,0:T(1,128)}, u32[]{:S(2)}) copy-start(f32[1,2048]{1,0:T(1,128)} %param.9) | copy-start | bytes 24580
  191.4 125.0 %all-to-all-start = ((bf16[32,36,2048]{2,1,0:T(8,128)(2,1)}), bf16[32,36,2048]{2,1,0:T(8,128)(2,1)}, u32[]{:S(2)}, u32[]{:S(2)}) async-start(bf16[32,36,2048]{2,1,0:T(8,128)(2,1)} %reshape.91), calls=%async_computation | async-start | bytes 10485760 | tf_op jit(solution)/shard_map/all_to_all | solution.py:81
  326.9 16.1 %collective-permute-start = (bf16[1,128,2048]{2,1,0:T(8,128)(2,1)S(1)}, bf16[1,128,2048]{2,1,0:T(8,128)(2,1)S(1)}, u32[]{:S(2)}, u32[]{:S(2)}) collective-permute-start(bf16[1,128,2048]{2,1,0:T(8,128)(2,1)S(1)} %fusion.10), channel_id=1, source_target_pairs={{0,32},{32,64},{64,96},{96,128},{128,160},{160,192},{192,224},{224... | collective-permute-start | bytes 1572872 | tf_op jit(solution)/shard_map/ppermute | solution.py:9
Sparse Core Ops, SparseCore 0:
  10.1 139.8 all-gather.2
where the time goes:
time: 352 us; the launch traced here: 351 us
  waiting for transfers between devices  216 us (61%)
  blocking collectives  44.4 us (13%)
  matrix products  32.9 us (9%)
  local copies, waits for them, and re-layouts  30.8 us (9%)
  between operations  13.5 us (4%)
  starting transfers between devices  7.39 us (2%)
  other arithmetic  5.4 us (2%)
    all_to_all x1, waiting for transfers between devices, local(): lax.all_to_all(owner_out.reshape(experts, capacity, model_width), 'expert...  116 us
    all_gather x1, waiting for transfers between devices, local(): gathered = lax.all_gather(normed, 'expert', axis=0, tiled=True)  85.4 us
    all_gather x1, blocking collectives, local(): table = lax.all_gather(route_local, 'expert', axis=0, tiled=True)  44.4 us
    ppermute x1, waiting for transfers between devices, shifted(): lax.ppermute(shard, axis, [(i, (i + by) % devices) for i in range(devices)])  14.5 us
    dot_general x1, matrix products, local(): jnp.einsum('btc,btd->bcd', selector, gathered.reshape(experts, tok_dev, m...  10.4 us
    reshape x1, local copies, waits for them, and re-layouts, local(): buffer.reshape(-1, model_width)  7.24 us
    reshape x1, local copies, waits for them, and re-layouts, local(): returned.reshape(experts * capacity, model_width)  7.22 us
    reshape x1, local copies, waits for them, and re-layouts, local(): owner_out.reshape(experts, capacity, model_width)  7.21 us
  transfers between devices with their start and end apart: 3, of which 3 were waited for; matrix products, arithmetic and copies ran while one was open for 4% of the time, Pallas kernels for 0%

commit v1 on v0

--- a/solution.py
+++ b/solution.py
@@ -55,8 +55,13 @@
     weights_map = jnp.sum(
         jnp.where(slot_hits, gate_values.astype(jnp.float32)[..., None], 0.0), axis=1
     ).astype(jnp.bfloat16)
-    table = lax.all_gather(route_local, "expert", axis=0, tiled=True)
-    gathered = lax.all_gather(normed, "expert", axis=0, tiled=True)
+    table, gathered = jnp.split(
+        lax.all_gather(
+            jnp.concatenate([route_local, normed], axis=1), "expert", axis=0, tiled=True
+        ),
+        [route_local.shape[1]],
+        axis=1,
+    )
     own_index = lax.axis_index("expert")
     flat_count = tok_dev * top_count
     blocks = table.reshape(experts, flat_count)

time: 352 us -> 387 us (1.099)
  waiting for transfers between devices: 216 us -> 276 us
  blocking collectives: 44.4 us -> 0 us
  local copies, waits for them, and re-layouts: 30.8 us -> 48.6 us
    all_gather x1, waiting for transfers between devices: 85.4 us -> 145 us  [local(): lax.all_gather(jnp.concatenate([route_local, normed], axis=1), 'expert',...]
    all_gather x1 -> x0, blocking collectives: 44.4 us -> none  [local(): table = lax.all_gather(route_local, 'expert', axis=0, tiled=True)]
    split x0 -> x1, local copies, waits for them, and re-layouts: none -> 17.6 us  [local(): jnp.split(lax.all_gather(jnp.concatenate([route_local, normed], axis=1),...]
  transfers between devices with their start and end apart: 3 -> 3, of which waited for: 3 -> 3; matrix products, arithmetic and copies ran while one was open for 4% -> 1% of each run, Pallas kernels for 0% -> 0%
where the time goes in v1:
time: 387 us; the launch traced here: 386 us
  waiting for transfers between devices  276 us (71%)
  local copies, waits for them, and re-layouts  48.6 us (13%)
  matrix products  32.9 us (9%)
  between operations  13.6 us (4%)
  starting transfers between devices  7.6 us (2%)
  other arithmetic  7.04 us (2%)
    all_gather x1, waiting for transfers between devices, local(): lax.all_gather(jnp.concatenate([route_local, normed], axis=1), 'expert',...  145 us
    all_to_all x1, waiting for transfers between devices, local(): lax.all_to_all(owner_out.reshape(experts, capacity, model_width), 'expert...  116 us
    split x1, local copies, waits for them, and re-layouts, local(): jnp.split(lax.all_gather(jnp.concatenate([route_local, normed], axis=1),...  17.6 us
    ppermute x1, waiting for transfers between devices, shifted(): lax.ppermute(shard, axis, [(i, (i + by) % devices) for i in range(devices)])  14.5 us
    dot_general x1, matrix products, local(): jnp.einsum('btc,btd->bcd', selector, gathered.reshape(experts, tok_dev, m...  10.4 us
  transfers between devices with their start and end apart: 3, of which 3 were waited for; matrix products, arithmetic and copies ran while one was open for 1% of the time, Pallas kernels for 0%

profile of v1, /device:TPU:2, one launch (start us, length us, event | category | flops | bytes accessed | tf_op | source)
XLA Modules:
  0.0 385.7 jit_solution(15136146183871686570)
XLA Ops:
  6.5 1.4 fusion.19
  7.9 0.8 copy.15
  8.7 1.3 fusion.21
  10.0 1.0 pad_maximum_fusion
  11.1 145.1 %all-gather.2.cloned.1.call-done = bf16[4096,2054]{1,0:T(8,128)(2,1)} async-done(((bf16[128,2054]{1,0:T(8,128)(2,1)}), bf16[4096,2054]{1,0:T(8,128)(2,1)}) %all-gather.2.cloned.1.call-update) | async-done | bytes 16826384 | tf_op jit(solution)/shard_map/all_gather | solution.py:59
  156.2 2.3 slice_compare_fusion
  158.5 2.5 eq.86
  161.1 1.0 fusion.14
  162.1 1.1 copy.20
  163.1 0.9 eq.87
  164.0 1.2 copy.21
  165.2 1.7 copy.19
  166.9 0.5 fusion.1
  167.4 17.6 %split.9 = bf16[4096,2048]{1,0:T(8,128)(2,1)} slice(bf16[4096,2054]{1,0:T(8,128)(2,1)} %all-gather.2.cloned.1.call-done), slice={[0:4096], [6:2054]} | slice | bytes 33554432 | tf_op jit(solution)/shard_map/split | solution.py:58
  185.0 10.4 %convolution_convert_fusion.1 = bf16[32,36,2048]{2,1,0:T(8,128)(2,1)} fusion(bf16[32,128,2048]{2,1,0:T(8,128)(2,1)} %bitcast.51, pred[32,128,36]{1,0,2:T(8,128)(4,1)S(1)} %fusion.1), kind=kOutput, calls=%fused_computation.1 | convolution fusion | flops 606339072 | bytes 21643264 | tf_op jit(solution)/shard_map/btc,btd->bcd/dot_general | solution.py:79
  195.4 7.2 %reshape.90 = bf16[1152,2048]{1,0:T(8,128)(2,1)} reshape(bf16[32,36,2048]{2,1,0:T(8,128)(2,1)} %convolution_convert_fusion.1) | data formatting | bytes 9437184 | tf_op jit(solution)/shard_map/reshape | solution.py:85
  202.6 6.8 %fusion.5 = f32[1152,768]{1,0:T(8,128)S(1)} fusion(bf16[1152,2048]{1,0:T(8,128)(2,1)} %reshape.90, bf16[1,1,2048,768]{3,2,1,0:T(8,128)(2,1)} %param.11), kind=kOutput, calls=%fused_computation.11 | convolution fusion | flops 3623878656 | bytes 11403264 | tf_op jit(solution)/shard_map/dot_general | solution.py:28
  209.4 4.2 %fusion.2 = bf16[1152,768]{1,0:T(8,128)(2,1)S(1)} fusion(bf16[1152,2048]{1,0:T(8,128)(2,1)S(1)} %copy-done.1, f32[1152,768]{1,0:T(8,128)S(1)} %fusion.5, bf16[1,1,2048,768]{3,2,1,0:T(8,128)(2,1)S(1)} %copy-done.6), kind=kOutput, calls=%fused_computation.8 | convolution fusion | flops 3629187072 | bytes 13172736 | tf_op jit(solution)/shard_map/dot_general | solution.py:29
  213.6 5.5 %convolution_convert_fusion = bf16[1152,2048]{1,0:T(8,128)(2,1)} fusion(bf16[1152,768]{1,0:T(8,128)(2,1)S(1)} %fusion.2, bf16[1,1,768,2048]{3,2,1,0:T(8,128)(2,1)S(1)} %copy-done), kind=kOutput, calls=%fused_computation | convolution fusion | flops 3626237952 | bytes 9633792 | tf_op jit(solution)/shard_map/dot_general | solution.py:31
  219.1 7.2 %reshape.91 = bf16[32,36,2048]{2,1,0:T(8,128)(2,1)} reshape(bf16[1152,2048]{1,0:T(8,128)(2,1)} %convolution_convert_fusion) | data formatting | bytes 9437184 | tf_op jit(solution)/shard_map/reshape | solution.py:87
  226.3 6.0 %all-to-all-start = ((bf16[32,36,2048]{2,1,0:T(8,128)(2,1)}), bf16[32,36,2048]{2,1,0:T(8,128)(2,1)}, u32[]{:S(2)}, u32[]{:S(2)}) async-start(bf16[32,36,2048]{2,1,0:T(8,128)(2,1)} %reshape.91), calls=%async_computation | async-start | bytes 10485760 | tf_op jit(solution)/shard_map/all_to_all | solution.py:86
  232.4 0.1 eq.73
  232.6 0.4 fusion.15
  232.9 0.1 convert_element_type.81
  233.1 1.5 fusion.18
  234.7 0.5 select_reduce_fusion
  235.2 116.2 %all-to-all-done = bf16[32,36,2048]{2,1,0:T(8,128)(2,1)} async-done(((bf16[32,36,2048]{2,1,0:T(8,128)(2,1)}), bf16[32,36,2048]{2,1,0:T(8,128)(2,1)}, u32[]{:S(2)}, u32[]{:S(2)}) %all-to-all-start) | async-done | bytes 4718624 | tf_op jit(solution)/shard_map/all_to_all | solution.py:86
  351.4 7.2 %reshape.92 = bf16[1152,2048]{1,0:T(8,128)(2,1)} reshape(bf16[32,36,2048]{2,1,0:T(8,128)(2,1)} %all-to-all-done) | data formatting | bytes 9437184 | tf_op jit(solution)/shard_map/reshape | solution.py:95
  358.6 3.3 fusion.10
  361.9 1.6 collective-permute-start
  363.5 14.5 %collective-permute-done = bf16[1,128,2048]{2,1,0:T(8,128)(2,1)S(1)} collective-permute-done((bf16[1,128,2048]{2,1,0:T(8,128)(2,1)S(1)}, bf16[1,128,2048]{2,1,0:T(8,128)(2,1)S(1)}, u32[]{:S(2)}, u32[]{:S(2)}) %collective-permute-start) | collective-permute-done | bytes 524320 | tf_op jit(solution)/shard_map/ppermute | solution.py:9
  378.0 0.8 copy.31
  (24 shorter events, 0.2 us)
Async XLA Ops:
  6.5 207.1 %copy-start = (bf16[1,1,768,2048]{3,2,1,0:T(8,128)(2,1)S(1)}, bf16[1,1,768,2048]{3,2,1,0:T(8,128)(2,1)}, u32[]{:S(2)}) copy-start(bf16[1,1,768,2048]{3,2,1,0:T(8,128)(2,1)} %param.13) | copy-start | bytes 9437188
  6.5 149.7 %all-gather.2.cloned.1.call-start = ((), (), s32[]{:S(2)}) async-start(), calls=%async_computation.1 | async-start | bytes 18382848 | tf_op jit(solution)/shard_map/all_gather | solution.py:59
  8.7 152.3 %copy-start.2 = (s32[1,128,6]{2,1,0:T(8,128)}, s32[1,128,6]{2,1,0:T(8,128)S(1)}, u32[]{:S(2)}) copy-start(s32[1,128,6]{2,1,0:T(8,128)S(1)} %copy.15) | copy-start | bytes 9220
  202.6 6.8 %copy-start.1 = (bf16[1152,2048]{1,0:T(8,128)(2,1)S(1)}, bf16[1152,2048]{1,0:T(8,128)(2,1)}, u32[]{:S(2)}) copy-start(bf16[1152,2048]{1,0:T(8,128)(2,1)} %reshape.90) | copy-start | bytes 14155780
  202.6 6.8 %copy-start.6 = (bf16[1,1,2048,768]{3,2,1,0:T(8,128)(2,1)S(1)}, bf16[1,1,2048,768]{3,2,1,0:T(8,128)(2,1)}, u32[]{:S(2)}) copy-start(bf16[1,1,2048,768]{3,2,1,0:T(8,128)(2,1)} %param.12) | copy-start | bytes 9437188
  226.3 6.0 %copy-start.4 = (s32[1,128,6]{1,0,2:T(1,128)S(1)}, s32[1,128,6]{1,0,2:T(1,128)}, u32[]{:S(2)}) copy-start(s32[1,128,6]{1,0,2:T(1,128)} %param.8) | copy-start | bytes 9220
  226.3 6.1 %copy-start.3 = (s32[1,128,6]{2,1,0:T(8,128)S(1)}, s32[1,128,6]{2,1,0:T(8,128)}, u32[]{:S(2)}) copy-start(s32[1,128,6]{2,1,0:T(8,128)} %copy-done.2) | copy-start | bytes 9220
  226.3 6.8 %copy-start.5 = (f32[1,2048]{1,0:T(1,128)S(1)}, f32[1,2048]{1,0:T(1,128)}, u32[]{:S(2)}) copy-start(f32[1,2048]{1,0:T(1,128)} %param.9) | copy-start | bytes 24580
  226.3 125.0 %all-to-all-start = ((bf16[32,36,2048]{2,1,0:T(8,128)(2,1)}), bf16[32,36,2048]{2,1,0:T(8,128)(2,1)}, u32[]{:S(2)}, u32[]{:S(2)}) async-start(bf16[32,36,2048]{2,1,0:T(8,128)(2,1)} %reshape.91), calls=%async_computation | async-start | bytes 10485760 | tf_op jit(solution)/shard_map/all_to_all | solution.py:86
  361.9 16.1 %collective-permute-start = (bf16[1,128,2048]{2,1,0:T(8,128)(2,1)S(1)}, bf16[1,128,2048]{2,1,0:T(8,128)(2,1)S(1)}, u32[]{:S(2)}, u32[]{:S(2)}) collective-permute-start(bf16[1,128,2048]{2,1,0:T(8,128)(2,1)S(1)} %fusion.10), channel_id=1, source_target_pairs={{0,32},{32,64},{64,96},{96,128},{128,160},{160,192},{192,224},{224... | collective-permute-start | bytes 1572872 | tf_op jit(solution)/shard_map/ppermute | solution.py:9
Sparse Core Ops, SparseCore 0:
  11.2 144.9 all-gather.1
